TPU v7x, 256 devices: a whole 4x4x8 slice. The times are simulated.
256 devices in a mesh: dp: 64 (over z, y, x_hi), mp: 4 (over x_lo, core).
Axes of the slice: x: 4 (x_hi: 2, x_lo: 2; x = x_hi * 2 + x_lo), y: 4, z: 8, core: 2. Of those that a mesh axis runs over, the one named last changes fastest.
Arguments:
- streams: bfloat16 [16384, 4, 8192], P('dp', None, 'mp'), may hold values from -200 to 200
- branch_out: bfloat16 [16384, 8192], P('dp', 'mp'), may hold values from -6 to 6
- merge_weight: float32 [20, 4, 8192], P(None, None, ('mp', 'dp')), may hold values from -0.03125 to 0.03125
- next_weight: float32 [24, 4, 8192], P(None, None, ('mp', 'dp')), may hold values from -0.03125 to 0.03125
- blend_bias: float32 [44], replicated, may hold values from -3 to 3
- blend_scale: float32 [5], replicated, may hold values from 0.5 to 3
- norm_gain: float32 [8192], P('mp'), may hold values from 0.5 to 1.5
Outputs:
- streams_out: bfloat16 [16384, 4, 8192], P('dp', None, 'mp')
- branch_in: bfloat16 [16384, 8192], P('dp', 'mp')
- next_mix: float32 [16384, 20], P('dp')
All inputs are finite; a program needn't handle non-finite values.
Results may differ from a plain program's by a relative error of at most 0.001.
Values sent between devices are 32-bit elements; how exact they have to be, the bound alone decides.
A program may use at most 64 MiB of HBM per device.

v0:
```python
import jax
import jax.numpy as jnp
from jax import lax
from jax.sharding import PartitionSpec as P

D = 8192
STREAMS = 4
BALANCE_ROUNDS = 6
epsilon = 1e-06


def copy_for_each(x, axis):
    peers = lax.axis_size(axis)
    return lax.all_to_all(jnp.broadcast_to(x[None], (peers, *x.shape)), axis, 0, 0, tiled=True)


def of_everyone(x, axis):
    everything = copy_for_each(x, axis)
    return jnp.sum(everything, axis=0)


def turned_gather(arrays, axis, dims):
    turned = [jnp.moveaxis(a, dim, 0) for a, dim in zip(arrays, dims)]
    both = jnp.concatenate([t.reshape(len(t), -1) for t in turned], axis=1)
    filled, at, gathered = (lax.all_gather(both, axis, axis=0, tiled=True), 0, [])
    for t, dim in zip(turned, dims):
        section = filled[:, at : at + t[0].size].reshape(-1, *t.shape[1:])
        gathered.append(jnp.moveaxis(section, 0, dim))
        at += t[0].size
    return tuple(gathered)


def balance_normalize(balanced_matrix):
    for balance_round in range(BALANCE_ROUNDS):
        balanced_matrix = balanced_matrix / jnp.sum(balanced_matrix, axis=2, keepdims=True)
        balanced_matrix = balanced_matrix / jnp.sum(balanced_matrix, axis=1, keepdims=True)
    return balanced_matrix


def settle(columns, finish):
    summed = of_everyone(columns, "mp")
    result = finish(summed)
    return result


def first_coef(raw_sums, squares, blend_bias, blend_scale):
    rms_root = jnp.sqrt(squares / (STREAMS * D) + epsilon)
    score_logits = raw_sums / rms_root[:, None]
    post_mix = 2.0 * jax.nn.sigmoid(blend_scale[0] * score_logits[:, :4] + blend_bias[:4])
    residual_blend = balance_normalize(
        jnp.exp(
            blend_scale[1] * score_logits[:, 4:20].reshape(-1, 4, 4)
            + blend_bias[4:20].reshape(4, 4)
        )
    )
    return (post_mix, residual_blend)


def second_coef(raw_sums, squares, blend_bias, blend_scale):
    rms_root = jnp.sqrt(squares / (STREAMS * D) + epsilon)
    score_logits = raw_sums / rms_root[:, None]
    pre_next = jax.nn.sigmoid(blend_scale[2] * score_logits[:, :4] + blend_bias[20:24])
    post_next = 2.0 * jax.nn.sigmoid(blend_scale[3] * score_logits[:, 4:8] + blend_bias[24:28])
    residual_following = balance_normalize(
        jnp.exp(
            blend_scale[4] * score_logits[:, 8:24].reshape(-1, 4, 4)
            + blend_bias[28:44].reshape(4, 4)
        )
    )
    return (pre_next, post_next, residual_following)


def mix_streams(residual_blend, post_mix, streams, branch_out):
    branch_wide = branch_out.astype(jnp.float32)
    outputs = []
    for target in range(STREAMS):
        total = post_mix[:, target, None] * branch_wide
        for source in range(STREAMS):
            total = total + residual_blend[:, target, source, None] * streams[:, source, :].astype(
                jnp.float32
            )
        outputs.append(total)
    return jnp.stack(outputs, axis=1)


def unite(pre_next, mixed):
    total = pre_next[:, 0, None] * mixed[:, 0, :]
    for source in range(1, STREAMS):
        total = total + pre_next[:, source, None] * mixed[:, source, :]
    return total


def local(streams, branch_out, merge_weight, next_weight, blend_bias, blend_scale, norm_gain):
    merge_rows, next_rows = turned_gather((merge_weight, next_weight), "dp", (2, 2))
    highest = lax.Precision.HIGHEST
    raw_part = jnp.einsum(
        "tic,kic->tk", streams, merge_rows, precision=highest, preferred_element_type=jnp.float32
    )
    gram_part = jnp.einsum("tic,tjc->tij", streams, streams, preferred_element_type=jnp.float32)
    columns = jnp.concatenate([raw_part, jnp.trace(gram_part, axis1=1, axis2=2)[:, None]], axis=1)

    def finish_first(summed):
        post_mix, residual_blend = first_coef(
            summed[:, :20], summed[:, 20], blend_bias, blend_scale
        )
        return jnp.concatenate([post_mix, residual_blend.reshape(-1, 16)], axis=1)

    merge_coef = settle(columns, finish_first)
    post_mix = merge_coef[:, :4]
    residual_blend = merge_coef[:, 4:20].reshape(-1, 4, 4)
    mixed = mix_streams(residual_blend, post_mix, streams, branch_out)
    streams_out = mixed.astype(jnp.bfloat16)
    raw_next = jnp.einsum("tic,kic->tk", mixed, next_rows, precision=highest)
    extra_cols = jnp.sum(mixed * mixed, axis=(1, 2))[:, None]
    columns_next = jnp.concatenate([raw_next, extra_cols], axis=1)

    def finish_second(summed):
        squares = summed[:, 24]
        pre_next, post_next, residual_following = second_coef(
            summed[:, :24], squares, blend_bias, blend_scale
        )
        pieces = [pre_next, post_next, residual_following.reshape(-1, 16)]
        return jnp.concatenate(pieces, axis=1)

    next_coef = settle(columns_next, finish_second)
    pre_next = next_coef[:, :4]
    next_mix = next_coef[:, 4:24]
    united = unite(pre_next, mixed)
    united_sq = of_everyone(jnp.sum(united * united, axis=1), "mp")
    branch_in = (united / jnp.sqrt(united_sq / D + epsilon)[:, None] * norm_gain).astype(
        jnp.bfloat16
    )
    return (streams_out, branch_in, next_mix)


def solution(mesh):
    placed = (
        P("dp", None, "mp"),
        P("dp", "mp"),
        P(None, None, ("mp", "dp")),
        P(None, None, ("mp", "dp")),
        P(),
        P(),
        P("mp"),
    )
    return jax.shard_map(
        local,
        mesh=mesh,
        in_specs=placed,
        out_specs=(P("dp", None, "mp"), P("dp", "mp"), P("dp", None)),
        check_vma=False,
    )
```

profile of v0, /device:TPU:1, one launch (start us, length us, event | category | flops | bytes accessed | tf_op | source)
XLA Modules:
  0.0 209.4 jit_solution(10708887090275913820)
XLA Ops:
  7.2 0.8 copy.64
  8.1 0.9 copy.65
  8.9 0.7 pad_maximum_fusion.4
  9.7 0.8 fusion.84
  10.6 6.7 %copy.68 = bf16[256,4,2048]{2,0,1:T(8,128)(2,1)} copy(bf16[256,4,2048]{2,1,0:T(4,128)(2,1)} %param.7) | data formatting | bytes 8388608 | tf_op args[0]
  17.4 5.8 %fusion.28 = f32[256]{0:T(256)S(1)} fusion(bf16[256,4,2048]{2,1,0:T(4,128)(2,1)S(1)} %copy-done.4, pred[4,4]{1,0:T(4,128)(4,1)S(1)} %iota_compare_fusion), kind=kOutput, calls=%fused_computation.54 | convolution fusion | flops 16785152 | bytes 4195344 | tf_op jit(solution)/shard_map/tic,tjc->tij/dot_general | solution.py:99
  23.1 107.6 %all-gather.2.cloned.1.call-done = f32[2048,176]{1,0:T(8,128)} async-done(((f32[32,176]{1,0:T(8,128)}), f32[2048,176]{1,0:T(8,128)}) %all-gather.2.cloned.1.call-update) | async-done | bytes 1441808 | tf_op jit(solution)/shard_map/all_gather | solution.py:25
  130.7 1.2 slice-done
  132.5 9.7 %convolution_bitcast_fusion = f32[256,20]{0,1:T(8,128)S(1)} fusion(f32[2048,20,4]{0,2,1:T(4,128)S(1)} %reshape.126, bf16[256,4,2048]{2,1,0:T(4,128)(2,1)} %param.7), kind=kOutput, calls=%fused_computation.56 | convolution fusion | flops 503316480 | bytes 4870144 | tf_op jit(solution)/shard_map/tic,kic->tk/dot_general | solution.py:96
  142.2 0.6 broadcast_in_dim.22
  142.8 7.7 %all-to-all-start = ((f32[4,256,21]{1,2,0:T(8,128)}), f32[4,256,21]{1,2,0:T(8,128)S(1)}, u32[]{:S(2)}, u32[]{:S(2)}) async-start(f32[4,256,21]{1,2,0:T(8,128)} %broadcast_in_dim.22), calls=%async_computation | async-start | bytes 196608 | tf_op jit(solution)/shard_map/all_to_all | solution.py:14
  150.5 0.6 fusion.82
  151.2 1.9 slice.249
  153.4 1.1 reshape.127
  155.2 0.8 fusion.60
  156.4 4.0 %fusion.13 = (f32[256,2048]{1,0:T(8,128)S(1)}, f32[256,2048]{1,0:T(8,128)S(1)}) fusion(bf16[256,2048]{1,0:T(8,128)(2,1)S(1)} %copy-done.5, f32[256]{0:T(256)S(1)} %bitcast.153, f32[256]{0:T(256)S(1)} %bitcast.154, f32[256]{0:T(256)S(1)} %bitcast.155, f32[256]{0:T(256)S(1)} %bitcast.148, f32[256]{0:T(256)S(1)} %bitcast.158, bf16[256,4,2048]{2,0,1:T(8,128)(2,1)} %copy.68, ...), kind=kLoop, calls=%fused_computation.35 | loop fusion | flops 12058624 | bytes 9447424 | tf_op jit(solution)/shard_map/add | solution.py:79
  160.4 2.3 %fusion.21 = (f32[256,2048]{1,0:T(8,128)S(1)}, f32[256,2048]{1,0:T(8,128)S(1)}) fusion(bf16[256,2048]{1,0:T(8,128)(2,1)S(1)} %copy-done.5, f32[256]{0:T(256)S(1)} %bitcast.144, f32[256]{0:T(256)S(1)} %bitcast.145, f32[256]{0:T(256)S(1)} %bitcast.146, f32[256]{0:T(256)S(1)} %bitcast.147, f32[256]{0:T(256)S(1)} %bitcast.157, ...), kind=kLoop, calls=%fused_computation.43 | loop fusion | flops 12058624 | bytes 9447424 | tf_op jit(solution)/shard_map/add | solution.py:79
  162.7 0.9 multiply_reduce_fusion
  163.9 0.7 copy-done.3
  164.6 6.6 %fusion.29 = f32[256,24]{0,1:T(8,128)S(1)} fusion(f32[256,1,2048]{2,0,1:T(8,128)S(1)} %bitcast.128, f32[256,1,2048]{2,0,1:T(8,128)S(1)} %bitcast.125, f32[256,1,2048]{2,0,1:T(8,128)S(1)} %bitcast.122, f32[256,1,2048]{2,0,1:T(8,128)S(1)} %bitcast.119, f32[2048,24,4]{0,2,1:T(4,128)S(1)} %copy-done.6), kind=kOutput, calls=%fused_computation.55 | convolution fusion | flops 610271232 | bytes 9199616 | tf_op jit(solution)/shard_map/tic,kic->tk/dot_general | solution.py:113
  171.3 0.7 broadcast_in_dim.24
  171.9 3.6 %all-to-all-start.1 = ((f32[4,256,25]{1,2,0:T(8,128)}), f32[4,256,25]{1,2,0:T(8,128)S(1)}, u32[]{:S(2)}, u32[]{:S(2)}) async-start(f32[4,256,25]{1,2,0:T(8,128)} %broadcast_in_dim.24), calls=%async_computation.1 | async-start | bytes 262144 | tf_op jit(solution)/shard_map/all_to_all | solution.py:14
  175.5 3.2 %fusion.27 = bf16[256,4,2048]{2,0,1:T(8,128)(2,1)S(1)} fusion(f32[256,1,2048]{2,0,1:T(8,128)} %bitcast.129, f32[256,1,2048]{2,0,1:T(8,128)} %bitcast.126, f32[256,1,2048]{2,0,1:T(8,128)} %bitcast.123, f32[256,1,2048]{2,0,1:T(8,128)S(1)} %bitcast.120), kind=kLoop, calls=%fused_computation.52 | loop fusion | flops 6291456 | bytes 12582912 | tf_op jit(solution)/shard_map/convert_element_type | solution.py:112
  178.8 5.3 %copy.76 = bf16[256,4,2048]{2,1,0:T(4,128)(2,1)} copy(bf16[256,4,2048]{2,0,1:T(8,128)(2,1)S(1)} %fusion.27) | data formatting | bytes 8388608
  184.1 1.3 fusion.49
  185.4 0.6 slice_multiply_fusion
  186.8 0.7 exponential_divide_fusion
  187.6 4.9 %multiply_reduce_fusion.1 = (f32[256]{0:T(256)S(1)}, f32[256,2048]{1,0:T(8,128)}) fusion(f32[256,2048]{1,0:T(8,128)} %copy-done.3, f32[256]{0:T(256)S(1)} %bitcast.161, f32[256,2048]{1,0:T(8,128)} %copy-done.2, f32[256]{0:T(256)S(1)} %bitcast.162, f32[256,2048]{1,0:T(8,128)} %copy-done.1, f32[256]{0:T(256)S(1)} %bitcast.163, ...), kind=kLoop, calls=%fused_computation.49 | loop fusion | flops 4718336 | bytes 10490880 | tf_op jit(solution)/shard_map/reduce_sum | solution.py:129
  193.1 3.5 %all-to-all-start.2 = ((f32[4,1,256]{2,1,0:T(1,128)}), f32[4,1,256]{2,1,0:T(1,128)S(1)}, u32[]{:S(2)}, u32[]{:S(2)}) async-start(f32[4,1,256]{2,1,0:T(1,128)} %broadcast_in_dim.25), calls=%async_computation.2 | async-start | bytes 8192 | tf_op jit(solution)/shard_map/all_to_all | solution.py:14
  196.5 0.6 pad_maximum_fusion.7
  197.2 2.5 %all-to-all-done.2 = f32[4,1,256]{2,1,0:T(1,128)S(1)} async-done(((f32[4,1,256]{2,1,0:T(1,128)}), f32[4,1,256]{2,1,0:T(1,128)S(1)}, u32[]{:S(2)}, u32[]{:S(2)}) %all-to-all-start.2) | async-done | bytes 4128 | tf_op jit(solution)/shard_map/all_to_all | solution.py:14
  199.7 2.9 %multiply_convert_fusion = bf16[256,2048]{1,0:T(8,128)(2,1)} fusion(f32[256,2048]{1,0:T(8,128)} %get-tuple-element.22, f32[2048]{0:T(1024)S(1)} %copy-done.9, f32[256]{0:T(256)S(1)} %add_sqrt_fusion), kind=kLoop, calls=%fused_computation.48 | loop fusion | flops 1572864 | bytes 3154944 | tf_op jit(solution)/shard_map/convert_element_type | solution.py:130
  (67 shorter events, 4.0 us)
Async XLA Ops:
  7.2 123.6 %all-gather.2.cloned.1.call-start = ((), (), s32[]{:S(2)}) async-start(), calls=%async_computation.3 | async-start | bytes 2129920 | tf_op jit(solution)/shard_map/all_gather | solution.py:25
  10.6 6.7 %copy-start.7 = (f32[44]{0:T(128)S(1)}, f32[44]{0:T(128)}, u32[]{:S(2)}) copy-start(f32[44]{0:T(128)} %param.11) | copy-start | bytes 532
  10.6 6.7 %copy-start.4 = (bf16[256,4,2048]{2,1,0:T(4,128)(2,1)S(1)}, bf16[256,4,2048]{2,1,0:T(4,128)(2,1)}, u32[]{:S(2)}) copy-start(bf16[256,4,2048]{2,1,0:T(4,128)(2,1)} %param.7) | copy-start | bytes 12582916
  130.7 1.2 slice-start
  132.5 18.1 %copy-start.8 = (f32[5]{0:T(128)S(1)}, f32[5]{0:T(128)}, u32[]{:S(2)}) copy-start(f32[5]{0:T(128)} %param.12) | copy-start | bytes 64
  142.8 11.7 %all-to-all-start = ((f32[4,256,21]{1,2,0:T(8,128)}), f32[4,256,21]{1,2,0:T(8,128)S(1)}, u32[]{:S(2)}, u32[]{:S(2)}) async-start(f32[4,256,21]{1,2,0:T(8,128)} %broadcast_in_dim.22), calls=%async_computation | async-start | bytes 196608 | tf_op jit(solution)/shard_map/all_to_all | solution.py:14
  153.4 2.9 %copy-start.5 = (bf16[256,2048]{1,0:T(8,128)(2,1)S(1)}, bf16[256,2048]{1,0:T(8,128)(2,1)}, u32[]{:S(2)}) copy-start(bf16[256,2048]{1,0:T(8,128)(2,1)} %param.8) | copy-start | bytes 3145732
  156.3 4.0 %copy-start = (bf16[256,4,2048]{2,0,1:T(8,128)(2,1)S(1)}, bf16[256,4,2048]{2,0,1:T(8,128)(2,1)}, u32[]{:S(2)}) copy-start(bf16[256,4,2048]{2,0,1:T(8,128)(2,1)} %copy.68) | copy-start | bytes 12582916
  160.3 3.2 %copy-start.1 = (f32[256,2048]{1,0:T(8,128)}, f32[256,2048]{1,0:T(8,128)S(1)}, u32[]{:S(2)}) copy-start(f32[256,2048]{1,0:T(8,128)S(1)} %get-tuple-element.26) | copy-start | bytes 6291460
  162.6 1.3 copy-start.2
  162.6 2.0 copy-start.3
  162.7 2.0 copy-start.6
  171.9 12.1 %all-to-all-start.1 = ((f32[4,256,25]{1,2,0:T(8,128)}), f32[4,256,25]{1,2,0:T(8,128)S(1)}, u32[]{:S(2)}, u32[]{:S(2)}) async-start(f32[4,256,25]{1,2,0:T(8,128)} %broadcast_in_dim.24), calls=%async_computation.1 | async-start | bytes 262144 | tf_op jit(solution)/shard_map/all_to_all | solution.py:14
  187.6 12.1 %copy-start.9 = (f32[2048]{0:T(1024)S(1)}, f32[2048]{0:T(1024)}, u32[]{:S(2)}) copy-start(f32[2048]{0:T(1024)} %param.13) | copy-start | bytes 24580
  193.1 6.6 %all-to-all-start.2 = ((f32[4,1,256]{2,1,0:T(1,128)}), f32[4,1,256]{2,1,0:T(1,128)S(1)}, u32[]{:S(2)}, u32[]{:S(2)}) async-start(f32[4,1,256]{2,1,0:T(1,128)} %broadcast_in_dim.25), calls=%async_computation.2 | async-start | bytes 8192 | tf_op jit(solution)/shard_map/all_to_all | solution.py:14
Sparse Core Ops, SparseCore 0:
  12.1 118.5 all-gather.1
where the time goes:
time: 210 us; the launch traced here: 209 us
  waiting for transfers between devices  110 us (52%)
  other arithmetic  24.6 us (12%)
  local copies, waits for them, and re-layouts  23.5 us (11%)
  matrix products  22.1 us (11%)
  starting transfers between devices  14.8 us (7%)
  between operations  14.4 us (7%)
    all_gather x1, waiting for transfers between devices, turned_gather(): lax.all_gather(both, axis, axis=0, tiled=True)  108 us
    all_to_all x3, starting transfers between devices, copy_for_each(): lax.all_to_all(jnp.broadcast_to(x[None], (peers, *x.shape)), axis, 0, 0,...  14.8 us
    unnamed x24, local copies, waits for them, and re-layouts  13 us
    dot_general x1, matrix products, local(): jnp.einsum('tic,kic->tk', streams, merge_rows, precision=highest, preferr...  9.68 us
    dot_general x1, matrix products, local(): raw_next = jnp.einsum('tic,kic->tk', mixed, next_rows, precision=highest)  6.63 us
    add x2, other arithmetic, mix_streams(): total + residual_blend[:, target, source, None] * streams[:, source, :].a...  6.25 us
    dot_general x1, matrix products, local(): jnp.einsum('tic,tjc->tij', streams, streams, preferred_element_type=jnp.f...  5.77 us
    reduce_sum x1, other arithmetic, local(): united_sq = of_everyone(jnp.sum(united * united, axis=1), 'mp')  4.89 us
  transfers between devices with their start and end apart: 4, of which 2 were waited for; matrix products, arithmetic and copies ran while one was open for 13% of the time, Pallas kernels for 0%

commit v1 on v0

--- a/solution.py
+++ b/solution.py
@@ -22,7 +22,19 @@
 def turned_gather(arrays, axis, dims):
     turned = [jnp.moveaxis(a, dim, 0) for a, dim in zip(arrays, dims)]
     both = jnp.concatenate([t.reshape(len(t), -1) for t in turned], axis=1)
-    filled, at, gathered = (lax.all_gather(both, axis, axis=0, tiled=True), 0, [])
+    filled, at, gathered = (
+        jnp.concatenate(
+            lax.all_to_all(
+                jnp.stack([both for _ in range(lax.psum(1, axis))], 0),
+                axis_name=axis,
+                concat_axis=0,
+                split_axis=0,
+            ),
+            0,
+        ),
+        0,
+        [],
+    )
     for t, dim in zip(turned, dims):
         section = filled[:, at : at + t[0].size].reshape(-1, *t.shape[1:])
         gathered.append(jnp.moveaxis(section, 0, dim))

time: 210 us -> 142 us (0.68)
  waiting for transfers between devices: 110 us -> 39.5 us
  starting transfers between devices: 14.8 us -> 31 us
  between operations: 14.4 us -> 1 us
    all_gather x1 -> x0, waiting for transfers between devices: 108 us -> none  [turned_gather(): lax.all_gather(both, axis, axis=0, tiled=True)]
    all_to_all x0 -> x1, waiting for transfers between devices: none -> 36.1 us  [turned_gather(): lax.all_to_all(jnp.stack([both for _ in range(lax.psum(1, axis))], 0), ax...]
    all_to_all x0 -> x1, starting transfers between devices: none -> 15.2 us  [turned_gather(): lax.all_to_all(jnp.stack([both for _ in range(lax.psum(1, axis))], 0), ax...]
  transfers between devices with their start and end apart: 4 -> 4, of which waited for: 2 -> 3; matrix products, arithmetic and copies ran while one was open for 13% -> 17% of each run, Pallas kernels for 0% -> 0%
where the time goes in v1:
time: 142 us; the launch traced here: 141 us
  waiting for transfers between devices  39.5 us (28%)
  starting transfers between devices  31 us (22%)
  other arithmetic  24 us (17%)
  local copies, waits for them, and re-layouts  23.5 us (17%)
  matrix products  22.1 us (16%)
    all_to_all x1, waiting for transfers between devices, turned_gather(): lax.all_to_all(jnp.stack([both for _ in range(lax.psum(1, axis))], 0), ax...  36.1 us
    all_to_all x3, starting transfers between devices, copy_for_each(): lax.all_to_all(jnp.broadcast_to(x[None], (peers, *x.shape)), axis, 0, 0,...  15.8 us
    all_to_all x1, starting transfers between devices, turned_gather(): lax.all_to_all(jnp.stack([both for _ in range(lax.psum(1, axis))], 0), ax...  15.2 us
    unnamed x24, local copies, waits for them, and re-layouts  13 us
    dot_general x1, matrix products, local(): jnp.einsum('tic,kic->tk', streams, merge_rows, precision=highest, preferr...  9.68 us
    dot_general x1, matrix products, local(): raw_next = jnp.einsum('tic,kic->tk', mixed, next_rows, precision=highest)  6.63 us
    add x2, other arithmetic, mix_streams(): total + residual_blend[:, target, source, None] * streams[:, source, :].a...  6.26 us
    dot_general x1, matrix products, local(): jnp.einsum('tic,tjc->tij', streams, streams, preferred_element_type=jnp.f...  5.77 us
  transfers between devices with their start and end apart: 4, of which 3 were waited for; matrix products, arithmetic and copies ran while one was open for 17% of the time, Pallas kernels for 0%

profile of v1, /device:TPU:1, one launch (start us, length us, event | category | flops | bytes accessed | tf_op | source)
XLA Modules:
  0.0 141.1 jit_solution(6994239515330747055)
XLA Ops:
  0.6 0.8 copy.78
  1.5 0.9 copy.79
  2.4 1.6 %stack.12 = f32[64,32,176]{2,1,0:T(8,128)} broadcast(f32[32,176]{1,0:T(8,128)S(1)} %pad_maximum_fusion.4), dimensions={1,2} | broadcast | bytes 1464320 | tf_op jit(solution)/shard_map/stack | solution.py:28
  4.0 15.2 %all-to-all-start = ((f32[64,32,176]{2,1,0:T(8,128)}), f32[64,32,176]{2,1,0:T(8,128)S(1)}, u32[]{:S(2)}, u32[]{:S(2)}) async-start(f32[64,32,176]{2,1,0:T(8,128)} %stack.12), calls=%async_computation | async-start | bytes 4194304 | tf_op jit(solution)/shard_map/all_to_all | solution.py:27
  19.5 6.7 %copy.82 = bf16[256,4,2048]{2,0,1:T(8,128)(2,1)} copy(bf16[256,4,2048]{2,1,0:T(4,128)(2,1)} %param.7) | data formatting | bytes 8388608 | tf_op args[0]
  26.3 5.8 %fusion.28 = f32[256]{0:T(256)S(1)} fusion(bf16[256,4,2048]{2,1,0:T(4,128)(2,1)S(1)} %copy-done.4, pred[4,4]{1,0:T(4,128)(4,1)S(1)} %iota_compare_fusion), kind=kOutput, calls=%fused_computation.54 | convolution fusion | flops 16785152 | bytes 4195344 | tf_op jit(solution)/shard_map/tic,tjc->tij/dot_general | solution.py:111
  32.1 36.1 %all-to-all-done = f32[64,32,176]{2,1,0:T(8,128)S(1)} async-done(((f32[64,32,176]{2,1,0:T(8,128)}), f32[64,32,176]{2,1,0:T(8,128)S(1)}, u32[]{:S(2)}, u32[]{:S(2)}) %all-to-all-start) | async-done | bytes 1441824 | tf_op jit(solution)/shard_map/all_to_all | solution.py:27
  68.2 1.2 copy.80
  69.4 1.3 reshape.132
  70.7 9.7 %convolution_bitcast_fusion = f32[256,20]{0,1:T(8,128)S(1)} fusion(f32[2048,20,4]{0,2,1:T(4,128)S(1)} %reshape.132, bf16[256,4,2048]{2,1,0:T(4,128)(2,1)} %param.7), kind=kOutput, calls=%fused_computation.56 | convolution fusion | flops 503316480 | bytes 4870144 | tf_op jit(solution)/shard_map/tic,kic->tk/dot_general | solution.py:108
  80.4 0.6 broadcast_in_dim.22
  81.0 8.1 %all-to-all-start.1 = ((f32[4,256,21]{1,2,0:T(8,128)}), f32[4,256,21]{1,2,0:T(8,128)S(1)}, u32[]{:S(2)}, u32[]{:S(2)}) async-start(f32[4,256,21]{1,2,0:T(8,128)} %broadcast_in_dim.22), calls=%async_computation.1 | async-start | bytes 196608 | tf_op jit(solution)/shard_map/all_to_all | solution.py:14
  89.1 0.6 fusion.82
  90.4 1.1 reshape.133
  91.5 0.9 all-to-all-done.1
  93.1 0.8 fusion.60
  94.2 4.0 %fusion.13 = (f32[256,2048]{1,0:T(8,128)S(1)}, f32[256,2048]{1,0:T(8,128)S(1)}) fusion(bf16[256,2048]{1,0:T(8,128)(2,1)S(1)} %copy-done.5, f32[256]{0:T(256)S(1)} %bitcast.156, f32[256]{0:T(256)S(1)} %bitcast.157, f32[256]{0:T(256)S(1)} %bitcast.158, f32[256]{0:T(256)S(1)} %bitcast.151, f32[256]{0:T(256)S(1)} %bitcast.161, bf16[256,4,2048]{2,0,1:T(8,128)(2,1)} %copy.82, ...), kind=kLoop, calls=%fused_computation.35 | loop fusion | flops 12058624 | bytes 9447424 | tf_op jit(solution)/shard_map/add | solution.py:91
  98.3 2.3 %fusion.21 = (f32[256,2048]{1,0:T(8,128)S(1)}, f32[256,2048]{1,0:T(8,128)S(1)}) fusion(bf16[256,2048]{1,0:T(8,128)(2,1)S(1)} %copy-done.5, f32[256]{0:T(256)S(1)} %bitcast.147, f32[256]{0:T(256)S(1)} %bitcast.148, f32[256]{0:T(256)S(1)} %bitcast.149, f32[256]{0:T(256)S(1)} %bitcast.150, f32[256]{0:T(256)S(1)} %bitcast.160, ...), kind=kLoop, calls=%fused_computation.43 | loop fusion | flops 12058624 | bytes 9447424 | tf_op jit(solution)/shard_map/add | solution.py:91
  100.6 0.9 multiply_reduce_fusion
  101.8 0.7 copy-done.3
  102.5 6.6 %fusion.29 = f32[256,24]{0,1:T(8,128)S(1)} fusion(f32[256,1,2048]{2,0,1:T(8,128)S(1)} %bitcast.129, f32[256,1,2048]{2,0,1:T(8,128)S(1)} %bitcast.126, f32[256,1,2048]{2,0,1:T(8,128)S(1)} %bitcast.123, f32[256,1,2048]{2,0,1:T(8,128)S(1)} %bitcast.120, f32[2048,24,4]{0,2,1:T(4,128)S(1)} %copy-done.6), kind=kOutput, calls=%fused_computation.55 | convolution fusion | flops 610271232 | bytes 9199616 | tf_op jit(solution)/shard_map/tic,kic->tk/dot_general | solution.py:125
  109.2 0.7 broadcast_in_dim.24
  109.8 4.2 %all-to-all-start.2 = ((f32[4,256,25]{1,2,0:T(8,128)}), f32[4,256,25]{1,2,0:T(8,128)S(1)}, u32[]{:S(2)}, u32[]{:S(2)}) async-start(f32[4,256,25]{1,2,0:T(8,128)} %broadcast_in_dim.24), calls=%async_computation.2 | async-start | bytes 262144 | tf_op jit(solution)/shard_map/all_to_all | solution.py:14
  114.1 3.2 %fusion.27 = bf16[256,4,2048]{2,0,1:T(8,128)(2,1)S(1)} fusion(f32[256,1,2048]{2,0,1:T(8,128)} %bitcast.130, f32[256,1,2048]{2,0,1:T(8,128)} %bitcast.127, f32[256,1,2048]{2,0,1:T(8,128)} %bitcast.124, f32[256,1,2048]{2,0,1:T(8,128)S(1)} %bitcast.121), kind=kLoop, calls=%fused_computation.52 | loop fusion | flops 6291456 | bytes 12582912 | tf_op jit(solution)/shard_map/convert_element_type | solution.py:124
  117.3 5.3 %copy.90 = bf16[256,4,2048]{2,1,0:T(4,128)(2,1)} copy(bf16[256,4,2048]{2,0,1:T(8,128)(2,1)S(1)} %fusion.27) | data formatting | bytes 8388608
  122.6 1.3 fusion.49
  124.0 0.6 slice_multiply_fusion
  125.4 0.7 exponential_divide_fusion
  126.1 4.9 %multiply_reduce_fusion.1 = (f32[256]{0:T(256)S(1)}, f32[256,2048]{1,0:T(8,128)}) fusion(f32[256,2048]{1,0:T(8,128)} %copy-done.3, f32[256]{0:T(256)S(1)} %bitcast.164, f32[256,2048]{1,0:T(8,128)} %copy-done.2, f32[256]{0:T(256)S(1)} %bitcast.165, f32[256,2048]{1,0:T(8,128)} %copy-done.1, f32[256]{0:T(256)S(1)} %bitcast.166, ...), kind=kLoop, calls=%fused_computation.49 | loop fusion | flops 4718336 | bytes 10490880 | tf_op jit(solution)/shard_map/reduce_sum | solution.py:141
  131.6 3.5 %all-to-all-start.3 = ((f32[4,1,256]{2,1,0:T(1,128)}), f32[4,1,256]{2,1,0:T(1,128)S(1)}, u32[]{:S(2)}, u32[]{:S(2)}) async-start(f32[4,1,256]{2,1,0:T(1,128)} %broadcast_in_dim.25), calls=%async_computation.3 | async-start | bytes 8192 | tf_op jit(solution)/shard_map/all_to_all | solution.py:14
  135.7 2.5 %all-to-all-done.3 = f32[4,1,256]{2,1,0:T(1,128)S(1)} async-done(((f32[4,1,256]{2,1,0:T(1,128)}), f32[4,1,256]{2,1,0:T(1,128)S(1)}, u32[]{:S(2)}, u32[]{:S(2)}) %all-to-all-start.3) | async-done | bytes 4128 | tf_op jit(solution)/shard_map/all_to_all | solution.py:14
  138.2 2.9 %multiply_convert_fusion = bf16[256,2048]{1,0:T(8,128)(2,1)} fusion(f32[256,2048]{1,0:T(8,128)} %get-tuple-element.25, f32[2048]{0:T(1024)S(1)} %copy-done.9, f32[256]{0:T(256)S(1)} %add_sqrt_fusion), kind=kLoop, calls=%fused_computation.48 | loop fusion | flops 1572864 | bytes 3154944 | tf_op jit(solution)/shard_map/convert_element_type | solution.py:142
  (66 shorter events, 4.6 us)
Async XLA Ops:
  4.0 15.2 %copy-start.7 = (f32[44]{0:T(128)S(1)}, f32[44]{0:T(128)}, u32[]{:S(2)}) copy-start(f32[44]{0:T(128)} %param.11) | copy-start | bytes 532
  4.0 64.1 %all-to-all-start = ((f32[64,32,176]{2,1,0:T(8,128)}), f32[64,32,176]{2,1,0:T(8,128)S(1)}, u32[]{:S(2)}, u32[]{:S(2)}) async-start(f32[64,32,176]{2,1,0:T(8,128)} %stack.12), calls=%async_computation | async-start | bytes 4194304 | tf_op jit(solution)/shard_map/all_to_all | solution.py:27
  19.5 6.7 %copy-start.4 = (bf16[256,4,2048]{2,1,0:T(4,128)(2,1)S(1)}, bf16[256,4,2048]{2,1,0:T(4,128)(2,1)}, u32[]{:S(2)}) copy-start(bf16[256,4,2048]{2,1,0:T(4,128)(2,1)} %param.7) | copy-start | bytes 12582916
  70.7 18.4 %copy-start.8 = (f32[5]{0:T(128)S(1)}, f32[5]{0:T(128)}, u32[]{:S(2)}) copy-start(f32[5]{0:T(128)} %param.12) | copy-start | bytes 64
  81.0 11.4 %all-to-all-start.1 = ((f32[4,256,21]{1,2,0:T(8,128)}), f32[4,256,21]{1,2,0:T(8,128)S(1)}, u32[]{:S(2)}, u32[]{:S(2)}) async-start(f32[4,256,21]{1,2,0:T(8,128)} %broadcast_in_dim.22), calls=%async_computation.1 | async-start | bytes 196608 | tf_op jit(solution)/shard_map/all_to_all | solution.py:14
  90.4 3.9 %copy-start.5 = (bf16[256,2048]{1,0:T(8,128)(2,1)S(1)}, bf16[256,2048]{1,0:T(8,128)(2,1)}, u32[]{:S(2)}) copy-start(bf16[256,2048]{1,0:T(8,128)(2,1)} %param.8) | copy-start | bytes 3145732
  94.2 4.0 %copy-start = (bf16[256,4,2048]{2,0,1:T(8,128)(2,1)S(1)}, bf16[256,4,2048]{2,0,1:T(8,128)(2,1)}, u32[]{:S(2)}) copy-start(bf16[256,4,2048]{2,0,1:T(8,128)(2,1)} %copy.82) | copy-start | bytes 12582916
  98.2 3.2 %copy-start.1 = (f32[256,2048]{1,0:T(8,128)}, f32[256,2048]{1,0:T(8,128)S(1)}, u32[]{:S(2)}) copy-start(f32[256,2048]{1,0:T(8,128)S(1)} %get-tuple-element.29) | copy-start | bytes 6291460
  100.5 1.3 copy-start.2
  100.6 2.0 %copy-start.3 = (f32[256,2048]{1,0:T(8,128)}, f32[256,2048]{1,0:T(8,128)S(1)}, u32[]{:S(2)}) copy-start(f32[256,2048]{1,0:T(8,128)S(1)} %get-tuple-element.31) | copy-start | bytes 6291460
  100.6 2.0 %copy-start.6 = (f32[2048,24,4]{0,2,1:T(4,128)S(1)}, f32[2048,24,4]{0,2,1:T(4,128)}, u32[]{:S(2)}) copy-start(f32[2048,24,4]{0,2,1:T(4,128)} %reshape.133) | copy-start | bytes 2359300
  109.8 12.7 %all-to-all-start.2 = ((f32[4,256,25]{1,2,0:T(8,128)}), f32[4,256,25]{1,2,0:T(8,128)S(1)}, u32[]{:S(2)}, u32[]{:S(2)}) async-start(f32[4,256,25]{1,2,0:T(8,128)} %broadcast_in_dim.24), calls=%async_computation.2 | async-start | bytes 262144 | tf_op jit(solution)/shard_map/all_to_all | solution.py:14
  126.1 12.1 %copy-start.9 = (f32[2048]{0:T(1024)S(1)}, f32[2048]{0:T(1024)}, u32[]{:S(2)}) copy-start(f32[2048]{0:T(1024)} %param.13) | copy-start | bytes 24580
  131.6 6.6 %all-to-all-start.3 = ((f32[4,1,256]{2,1,0:T(1,128)}), f32[4,1,256]{2,1,0:T(1,128)S(1)}, u32[]{:S(2)}, u32[]{:S(2)}) async-start(f32[4,1,256]{2,1,0:T(1,128)} %broadcast_in_dim.25), calls=%async_computation.3 | async-start | bytes 8192 | tf_op jit(solution)/shard_map/all_to_all | solution.py:14
